TPU v7x, 32 devices: a whole 2x2x4 slice. The times are simulated.
32 devices in a mesh: head: 4 (over y, x), seq: 8 (over z, core).
Axes of the slice: x: 2, y: 2, z: 4, core: 2. Of those that a mesh axis runs over, the one named last changes fastest.
Arguments:
- tokens: float32 [8, 1024, 1024], P('seq', 'head'), may hold values from -6 to 6
- patch_counts: int32 [8], P('seq'), may hold values from 256 to 874, as said below
- w_qkv: bfloat16 [1024, 3072], P(('head', 'seq')), may hold values from -0.1875 to 0.1875
- w_out: bfloat16 [1024, 1024], P(('head', 'seq')), may hold values from -3.453125 to 3.453125
- w_up: bfloat16 [1024, 4096], P(('head', 'seq')), may hold values from -0.1875 to 0.1875
- w_down: bfloat16 [4096, 1024], P(('head', 'seq')), may hold values from -0.09375 to 0.09375
- w_patch: bfloat16 [1024, 1024], P(('head', 'seq')), may hold values from -0.1875 to 0.1875
- w_class: bfloat16 [1024, 1024], P(('head', 'seq')), may hold values from -0.1875 to 0.1875
- norm_gains: bfloat16 [2, 1024], P(None, ('head', 'seq')), may hold values from 0.099609375 to 1.8984375
- mask_norm: float32 [2, 150], replicated, may hold values from 0.5 to 1.5
- grad_masks: float32 [8, 1024, 150], P('seq', 'head'), may hold values from -6 to 6
Outputs:
- class_masks: float32 [8, 1024, 150], P('seq', 'head')
- grad_tokens: float32 [8, 1024, 1024], P('seq', 'head')
- grad_w_qkv: float32 [1024, 3072], P(('head', 'seq'))
- grad_w_out: float32 [1024, 1024], P(('head', 'seq'))
- grad_w_up: float32 [1024, 4096], P(('head', 'seq'))
- grad_w_down: float32 [4096, 1024], P(('head', 'seq'))
- grad_w_patch: float32 [1024, 1024], P(('head', 'seq'))
- grad_w_class: float32 [1024, 1024], P(('head', 'seq'))
- grad_norm_gains: float32 [2, 1024], P(None, ('head', 'seq'))
- grad_mask_norm: float32 [2, 150], replicated
Inputs may be any that keep to these rules, and one draw needn't show every extreme that they name: An image's slot holds its 150 class rows first, then patch_counts[i] patch rows, then padding; some image has 874 patches and some 1024 // 4.
All inputs are finite; a program needn't handle non-finite values.
Results may differ from a plain program's by a relative error of at most 0.02.
Values may be sent and summed in bfloat16 or wider, within the bound.
A program may use at most 192 MiB of HBM per device.

v0:
```python
from functools import partial

import jax
import jax.numpy as jnp
from jax import lax
from jax.experimental import pallas as pl
from jax.experimental.pallas import tpu as pltpu
from jax.sharding import PartitionSpec as P

HEADS = 16
DH = 64
CLS = 150


def spread_2(value, axis, source):
    kept = jnp.where(lax.axis_index(axis) == source, value, 0).astype(value.dtype)
    return lax.psum(kept, axis)


def standardize(values):
    center = values - jnp.mean(values, axis=-1, keepdims=True)
    inverse = lax.rsqrt(jnp.mean(center * center, axis=-1, keepdims=True) + 1e-05)
    return (center * inverse, inverse)


def standard_back(normal, inverse, upstream):
    middle = jnp.mean(upstream, axis=-1, keepdims=True)
    along = jnp.mean(upstream * normal, axis=-1, keepdims=True)
    return inverse * (upstream - middle - normal * along)


def unit_scale(values):
    return lax.rsqrt(jnp.sum(values * values, axis=-1, keepdims=True) + 1e-06)


def unit_back(values, upstream):
    factor = unit_scale(values)
    direct = values * factor
    return factor * (upstream - direct * jnp.sum(upstream * direct, axis=-1, keepdims=True))


def block_scores(query_block, key_rows, key_live, scaling):
    scores = (
        jnp.einsum("qd,kd->qk", query_block, key_rows, preferred_element_type=jnp.float32) * scaling
    )
    return jnp.where(key_live, scores, -1e30)


def attend_head(queries, key_rows, values, key_live, scaling, blocks):
    head_width = queries.shape[-1]

    def single(query_block):
        scores = block_scores(query_block, key_rows, key_live, scaling)
        highest = jnp.max(scores, axis=-1, keepdims=True)
        weights_raw = jnp.exp(scores - highest)
        totals = jnp.sum(weights_raw, axis=-1, keepdims=True)
        weights = (weights_raw / totals).astype(jnp.bfloat16)
        output = jnp.einsum("qk,kd->qd", weights, values, preferred_element_type=jnp.float32)
        return (output.astype(jnp.bfloat16), (highest + jnp.log(totals))[:, 0])

    outputs, logsum = lax.map(single, queries.reshape(blocks, -1, head_width))
    return (outputs.reshape(-1, head_width), logsum.reshape(-1))


def attend_back(queries, key_rows, values, grad_out, logsum, key_live, scaling, blocks):
    head_width = queries.shape[-1]

    def single(running, pieces):
        grad_keys, grad_values = running
        query_block, grad_block, logsum_block = pieces
        scores = block_scores(query_block, key_rows, key_live, scaling)
        weights = jnp.exp(scores - logsum_block[:, None])
        grad_values = grad_values + jnp.einsum(
            "qk,qd->kd",
            weights.astype(jnp.bfloat16),
            grad_block,
            preferred_element_type=jnp.float32,
        )
        grad_weights = jnp.einsum(
            "qd,kd->qk", grad_block, values, preferred_element_type=jnp.float32
        )
        deltas = jnp.sum(grad_weights * weights, axis=-1, keepdims=True)
        grad_scores = (weights * (grad_weights - deltas)).astype(jnp.bfloat16)
        grad_query = (
            jnp.einsum("qk,kd->qd", grad_scores, key_rows, preferred_element_type=jnp.float32)
            * scaling
        )
        grad_keys = (
            grad_keys
            + jnp.einsum("qk,qd->kd", grad_scores, query_block, preferred_element_type=jnp.float32)
            * scaling
        )
        return ((grad_keys, grad_values), grad_query)

    zero_state = jnp.zeros(key_rows.shape, jnp.float32)
    pieces = (
        queries.reshape(blocks, -1, head_width),
        grad_out.reshape(blocks, -1, head_width),
        logsum.reshape(blocks, -1),
    )
    (grad_keys, grad_values), grad_queries = lax.scan(single, (zero_state, zero_state), pieces)
    return (grad_queries.reshape(-1, head_width), grad_keys, grad_values)


def body_general(
    tokens,
    patch_counts,
    w_qkv,
    w_out,
    w_up,
    w_down,
    w_patch,
    w_class,
    norm_gains,
    mask_norm,
    grad_masks,
):
    gains_rows = norm_gains.T
    gathered = (
        lax.all_gather(w_qkv, ("head", "seq"), axis=0, tiled=True),
        lax.all_gather(w_out, ("head", "seq"), axis=0, tiled=True),
        lax.all_gather(w_up, ("head", "seq"), axis=0, tiled=True),
        lax.all_gather(w_down, ("head", "seq"), axis=0, tiled=True),
        lax.all_gather(w_patch, ("head", "seq"), axis=0, tiled=True),
        lax.all_gather(w_class, ("head", "seq"), axis=0, tiled=True),
        lax.all_gather(gains_rows, ("head", "seq"), axis=0, tiled=True),
    )
    full_qkv, full_out, full_up, full_down, full_patch, full_class, full_gains = gathered
    gain_one = full_gains[:, 0].astype(jnp.float32)
    gain_two = full_gains[:, 1].astype(jnp.float32)
    image_count = tokens.shape[0]
    row_count = tokens.shape[1]
    groups = lax.axis_size("head")
    slot_rows = row_count * groups
    local_heads = HEADS // groups
    position = lax.axis_index("head") * row_count + jnp.arange(row_count, dtype=jnp.int32)
    live_limit = CLS + patch_counts
    patch_rows = ((position[None, :] >= CLS) & (position[None, :] < live_limit[:, None])).astype(
        jnp.float32
    )[:, :, None]
    key_live = (jnp.arange(slot_rows, dtype=jnp.int32)[None, :] < live_limit[:, None])[:, None, :]
    root_flag = (lax.axis_index("head") == 0).astype(jnp.float32)
    scaling = DH ** (-0.5)
    blocks = slot_rows // 512
    normal_one, inverse_one = standardize(tokens)
    normed_one = (normal_one * gain_one).astype(jnp.bfloat16)
    triple = jnp.einsum(
        "ird,dt->irt", normed_one, full_qkv, preferred_element_type=jnp.float32
    ).astype(jnp.bfloat16)
    spread = lax.all_to_all(triple, "head", split_axis=2, concat_axis=1, tiled=True).reshape(
        image_count, slot_rows, local_heads, 3, DH
    )
    image = 0
    outputs = []
    image_logsums = []
    for number in range(local_heads):
        output, logsum = attend_head(
            spread[image, :, number, 0],
            spread[image, :, number, 1],
            spread[image, :, number, 2],
            key_live[image],
            scaling,
            blocks,
        )
        outputs.append(output)
        image_logsums.append(logsum)
    image_outputs = [jnp.stack(outputs, axis=1).reshape(slot_rows, local_heads * DH)]
    logsums = [image_logsums]
    attended_heads = jnp.stack(image_outputs, axis=0)
    attended = lax.all_to_all(attended_heads, "head", split_axis=1, concat_axis=2, tiled=True)
    second = tokens + jnp.einsum(
        "ire,ed->ird", attended, full_out, preferred_element_type=jnp.float32
    )
    normal_two, inverse_two = standardize(second)
    normed_two = (normal_two * gain_two).astype(jnp.bfloat16)
    hidden = jnp.einsum("ird,df->irf", normed_two, full_up, preferred_element_type=jnp.float32)
    gelu_exact = partial(jax.nn.gelu, approximate=False)
    active = gelu_exact(hidden).astype(jnp.bfloat16)
    residual = second + jnp.einsum(
        "irf,fd->ird", active, full_down, preferred_element_type=jnp.float32
    )
    rounded = residual.astype(jnp.bfloat16)
    patch_proj = jnp.einsum("ird,de->ire", rounded, full_patch, preferred_element_type=jnp.float32)
    patch_unit = (patch_proj * unit_scale(patch_proj)).astype(jnp.bfloat16)
    class_proj = jnp.einsum(
        "ird,de->ire", rounded[:, :CLS], full_class, preferred_element_type=jnp.float32
    )
    class_unit = (class_proj * unit_scale(class_proj)).astype(jnp.bfloat16)
    classes = spread_2(class_unit, "head", 0)
    products = jnp.einsum("ird,icd->irc", patch_unit, classes, preferred_element_type=jnp.float32)
    normal_mask, inverse_mask = standardize(products)
    class_masks = (normal_mask * mask_norm[0] + mask_norm[1]) * patch_rows
    upstream = grad_masks * patch_rows
    norm_grads = lax.psum(
        jnp.stack([jnp.sum(upstream * normal_mask, axis=(0, 1)), jnp.sum(upstream, axis=(0, 1))]),
        ("head", "seq"),
    )
    d_products = standard_back(normal_mask, inverse_mask, upstream * mask_norm[0]).astype(
        jnp.bfloat16
    )
    d_patch_unit = jnp.einsum(
        "irc,icd->ird", d_products, classes, preferred_element_type=jnp.float32
    )
    class_part = jnp.einsum(
        "irc,ird->icd", d_products, patch_unit, preferred_element_type=jnp.float32
    )
    d_class_unit = lax.psum(class_part.astype(jnp.bfloat16), "head").astype(jnp.float32)
    d_patch_proj = unit_back(patch_proj, d_patch_unit).astype(jnp.bfloat16)
    d_class_proj = (unit_back(class_proj, d_class_unit) * root_flag).astype(jnp.bfloat16)
    regathered = (
        lax.all_gather(w_qkv, ("head", "seq"), axis=0, tiled=True),
        lax.all_gather(w_out, ("head", "seq"), axis=0, tiled=True),
        lax.all_gather(w_up, ("head", "seq"), axis=0, tiled=True),
        lax.all_gather(w_down, ("head", "seq"), axis=0, tiled=True),
        lax.all_gather(w_patch, ("head", "seq"), axis=0, tiled=True),
        lax.all_gather(w_class, ("head", "seq"), axis=0, tiled=True),
        lax.all_gather(gains_rows, ("head", "seq"), axis=0, tiled=True),
    )
    back_qkv, back_out, back_up, back_down, back_patch, back_class, back_gains = regathered
    back_one = back_gains[:, 0].astype(jnp.float32)
    back_two = back_gains[:, 1].astype(jnp.float32)
    grad_patch = jnp.einsum(
        "ird,ire->de", rounded, d_patch_proj, preferred_element_type=jnp.float32
    )
    grad_class = jnp.einsum(
        "ird,ire->de", rounded[:, :CLS], d_class_proj, preferred_element_type=jnp.float32
    )
    d_residual = jnp.einsum(
        "ire,de->ird", d_patch_proj, back_patch, preferred_element_type=jnp.float32
    )
    class_term = jnp.einsum(
        "ire,de->ird", d_class_proj, back_class, preferred_element_type=jnp.float32
    )
    d_residual = d_residual.at[:, :CLS].add(class_term)
    d_branch = d_residual.astype(jnp.bfloat16)
    grad_down = jnp.einsum("irf,ird->fd", active, d_branch, preferred_element_type=jnp.float32)
    d_active = jnp.einsum("ird,fd->irf", d_branch, back_down, preferred_element_type=jnp.float32)
    gelu_pull = jax.vjp(gelu_exact, hidden)[1]
    d_hidden = gelu_pull(d_active)[0].astype(jnp.bfloat16)
    grad_up = jnp.einsum("ird,irf->df", normed_two, d_hidden, preferred_element_type=jnp.float32)
    d_normed_two = jnp.einsum("irf,df->ird", d_hidden, back_up, preferred_element_type=jnp.float32)
    d_second = d_residual + standard_back(normal_two, inverse_two, d_normed_two * back_two)
    grad_gain_two = jnp.sum(d_normed_two * normal_two, axis=(0, 1))
    d_mix = d_second.astype(jnp.bfloat16)
    grad_out = jnp.einsum("ire,ird->ed", attended, d_mix, preferred_element_type=jnp.float32)
    d_attended = jnp.einsum(
        "ird,ed->ire", d_mix, back_out, preferred_element_type=jnp.float32
    ).astype(jnp.bfloat16)
    d_heads = lax.all_to_all(d_attended, "head", split_axis=2, concat_axis=1, tiled=True).reshape(
        image_count, slot_rows, local_heads, DH
    )
    image = 0
    head_grads = []
    for number in range(local_heads):
        grad_queries, grad_keys, grad_values = attend_back(
            spread[image, :, number, 0],
            spread[image, :, number, 1],
            spread[image, :, number, 2],
            d_heads[image, :, number],
            logsums[image][number],
            key_live[image],
            scaling,
            blocks,
        )
        head_grads.append(jnp.stack([grad_queries, grad_keys, grad_values], axis=1))
    image_grads = [jnp.stack(head_grads, axis=1).reshape(slot_rows, local_heads * 3 * DH)]
    d_spread = jnp.stack(image_grads, axis=0).astype(jnp.bfloat16)
    d_triple = lax.all_to_all(d_spread, "head", split_axis=1, concat_axis=2, tiled=True)
    grad_qkv = jnp.einsum("ird,irt->dt", normed_one, d_triple, preferred_element_type=jnp.float32)
    d_normed_one = jnp.einsum("irt,dt->ird", d_triple, back_qkv, preferred_element_type=jnp.float32)
    grad_inputs = d_second + standard_back(normal_one, inverse_one, d_normed_one * back_one)
    grad_gain_one = jnp.sum(d_normed_one * normal_one, axis=(0, 1))
    grad_gains = jnp.stack([grad_gain_one, grad_gain_two], axis=1)
    reduced = (
        lax.psum_scatter(grad_qkv, ("head", "seq"), scatter_dimension=0, tiled=True),
        lax.psum_scatter(grad_out, ("head", "seq"), scatter_dimension=0, tiled=True),
        lax.psum_scatter(grad_up, ("head", "seq"), scatter_dimension=0, tiled=True),
        lax.psum_scatter(grad_down, ("head", "seq"), scatter_dimension=0, tiled=True),
        lax.psum_scatter(grad_patch, ("head", "seq"), scatter_dimension=0, tiled=True),
        lax.psum_scatter(grad_class, ("head", "seq"), scatter_dimension=0, tiled=True),
        lax.psum_scatter(grad_gains, ("head", "seq"), scatter_dimension=0, tiled=True),
    )
    return (
        class_masks,
        grad_inputs,
        reduced[0],
        reduced[1],
        reduced[2],
        reduced[3],
        reduced[4],
        reduced[5],
        reduced[6].T,
        norm_grads,
    )


MESH = pl.DeviceIdType.MESH
LOG2E = 1.4426950408889634
SLOTS = 16
FRONT_COPIES = 160
REAR_COPIES = 88


def matmul(left, right):
    return jnp.dot(left, right, preferred_element_type=jnp.float32)


def matmul_nt(left, right):
    return lax.dot_general(left, right, (((1,), (1,)), ((), ())), preferred_element_type=jnp.float32)


def matmul_tn(left, right):
    return lax.dot_general(left, right, (((0,), (0,)), ((), ())), preferred_element_type=jnp.float32)


def norm(values):
    center = values - jnp.mean(values, axis=-1, keepdims=True)
    inverse = lax.rsqrt(jnp.mean(center * center, axis=-1, keepdims=True) + 1e-05)
    return center * inverse, inverse


def device(y, x, z, c):
    return (y * 2 + x, z * 2 + c)


class Links:
    def __init__(self, send_sem, recv_sem):
        head, seq = lax.axis_index("head"), lax.axis_index("seq")
        self.y, self.x, self.z, self.c = head // 2, head % 2, seq // 2, seq % 2
        y, x, z, c = self.y, self.x, self.z, self.c
        self.sibling = device(y, x, z, 1 - c)
        self.along_x = device(y, 1 - x, z, c)
        self.along_y = device(1 - y, x, z, c)
        self.across = device(1 - y, 1 - x, z, c)
        self.along_z = [device(y, x, (z + k) % 4, c) for k in (1, 2, 3)]
        self.send_sem, self.recv_sem, self.count, self.made, self.lines = send_sem, recv_sem, 0, [], []

    def greet(self):
        barrier = pltpu.get_barrier_semaphore()
        peers = [self.sibling, self.along_x, self.along_y, self.across] + self.along_z
        for peer in peers:
            pl.semaphore_signal(barrier, inc=1, device_id=peer, device_id_type=MESH)
        pl.semaphore_wait(barrier, len(peers))

    def plan(self, source, target, peer, sends=None, again=False):
        number = self.count - again
        self.count = number + 1
        copy = pltpu.make_async_remote_copy(
            src_ref=source,
            dst_ref=target,
            send_sem=self.send_sem.at[number],
            recv_sem=self.recv_sem.at[number],
            device_id=peer,
            device_id_type=MESH,
        )
        if not again:
            self.made.append((copy, sends))
        return copy

    def drain(self):
        for copy, sends in self.made:
            if sends is None:
                copy.wait_send()
            else:
                pl.when(sends)(copy.wait_send)
        for line in self.lines:
            line.drain()


class Stage:
    def __init__(self, links, moves, again=False):
        self.copies = [links.plan(*move, again=again) for move in moves]

    def start(self):
        for copy in self.copies:
            copy.start()

    def wait(self):
        for copy in self.copies:
            copy.wait_recv()


class Line:
    def __init__(self, links, piece, source=None):
        self.links, self.piece = links, piece
        self.source = piece(links.z) if source is None else source
        self.base = links.count
        links.count += 5
        links.lines.append(self)

    def copy(self, source, target, sent, landed):
        links = self.links
        return pltpu.make_async_remote_copy(
            src_ref=source,
            dst_ref=self.piece(landed),
            send_sem=links.send_sem.at[self.base + sent],
            recv_sem=links.recv_sem.at[self.base + landed],
            device_id=device(links.y, links.x, target, links.c),
            device_id_type=MESH,
        )

    def direct(self, target):
        z = self.links.z
        return (z != target) if target in (1, 2) else (z != target) & (z != 3 - target)

    def start(self):
        for target in (1, 2, 0, 3):

            @pl.when(self.direct(target))
            def _(target=target):
                self.copy(self.source, target, target, self.links.z).start()

    def relay(self):
        for at, end in ((2, 0), (1, 3)):

            @pl.when(self.links.z == at)
            def _(end=end):
                self.copy(self.source, 3 - end, 4, end).wait_recv()
                self.copy(self.piece(end), 3 - end, 4, end).start()

    def wait(self):
        z = self.links.z
        for origin in range(4):
            pending = z != origin
            if origin in (0, 3):
                pending = pending & (z != (2 if origin == 0 else 1))

            @pl.when(pending)
            def _(origin=origin):
                self.copy(self.source, 0, 0, origin).wait_recv()

    def drain(self):
        for target in range(4):

            @pl.when(self.direct(target))
            def _(target=target):
                self.copy(self.source, target, target, self.links.z).wait_send()

        @pl.when((self.links.z == 1) | (self.links.z == 2))
        def _():
            self.copy(self.source, 0, 4, 0).wait_send()


def at_slots(slot, events):
    for number, event in events.items():
        pl.when(slot == number)(event)


def weight_gradient(target, left, right):
    per = left.shape[1] // 4
    for j in range(4):
        piece = matmul_tn(left[:, j * per : (j + 1) * per], right[...]).astype(jnp.bfloat16)
        if len(target.shape) == 6:
            target[j // 2, j % 2] = piece.reshape(target.shape[2:])
        else:
            pair = target.shape[1] // 2
            at = (j % 2) * pair
            target[j // 2, at : at + pair] = piece.reshape((pair,) + target.shape[2:])


class LineSum:
    def __init__(self, links, piece, got):
        self.links, self.piece, self.got = links, piece, got
        self.base = links.count
        links.count += 5
        links.lines.append(self)

    def copy(self, piece, target, slot, sent):
        links = self.links
        return pltpu.make_async_remote_copy(
            src_ref=self.piece(piece),
            dst_ref=self.got.at[slot],
            send_sem=links.send_sem.at[self.base + sent],
            recv_sem=links.recv_sem.at[self.base + slot],
            device_id=device(links.y, links.x, target, links.c),
            device_id_type=MESH,
        )

    def start(self):
        z = self.links.z
        for target, end, middle in ((3, 0, 1), (0, 3, 2)):

            @pl.when(z == end)
            def _(target=target, middle=middle):
                self.copy(target, middle, 4, target).start()

        for target in range(4):
            direct = z != target
            if target in (0, 3):
                direct = z == (1 if target == 0 else 2)

            @pl.when(direct)
            def _(target=target):
                self.copy(target, target, z, target).start()

    def relay(self):
        z = self.links.z
        for target, middle in ((3, 1), (0, 2)):

            @pl.when(z == middle)
            def _(target=target, middle=middle):
                self.copy(target, target, 4, target).wait_recv()
                own = self.piece(target)
                own[...] = own[...] + self.got[4]
                self.copy(target, target, middle, target).start()

    def collect(self, add):
        z = self.links.z
        for origin in range(4):
            comes = z != origin
            if origin in (0, 3):
                comes = comes & (z != 3 - origin)

            @pl.when(comes)
            def _(origin=origin):
                self.copy(0, 0, origin, 0).wait_recv()
                add(origin)

    def drain(self):
        for target in range(4):

            @pl.when(self.links.z != target)
            def _(target=target):
                self.copy(target, target, 0, target).wait_send()


class Sum:
    def __init__(self, links, partial_ref, sib, one, two, three, kind):
        y, x, z, c = links.y, links.x, links.z, links.c
        self.links, self.sib, self.one, self.two, self.three = links, sib, one, two, three
        self.kind = kind
        self.q = y * (1 - c) + x * c
        lead = () if kind == "down" else (slice(None),) * 3
        total = self.total = partial_ref.at[(*lead, c)]
        self.core = Stage(links, [(partial_ref.at[(*lead, 1 - c)], sib, links.sibling)])
        if kind in ("up_y", "all_y"):
            self.first = Stage(links, [(total.at[1 - y], one, links.along_y)])
            self.kept = lambda i, j: (y, i, j)
        elif kind in ("up_x", "all_x"):
            self.first = Stage(links, [(total.at[:, 1 - x], one, links.along_x)])
            self.kept = lambda i, j: (i, x, j)
        else:
            turned = device(y + (1 - c) * (1 - 2 * y), x + c * (1 - 2 * x), z, c)
            self.first = Stage(links, [(total.at[1 - self.q], one, turned)])
            self.line = LineSum(links, lambda at: total.at[self.q, at], three)
        if kind == "up_y":
            self.line = LineSum(links, lambda at: total.at[y, :, at], three)
            self.last = Stage(links, [(total.at[y, 1 - x, z], two, links.along_x)])
        elif kind == "up_x":
            self.line = LineSum(links, lambda at: total.at[:, x, at], three)
            self.last = Stage(links, [(total.at[1 - y, x, z], two, links.along_y)])
        elif kind == "all_x":
            self.second = Stage(links, [(total.at[1 - y, x], two, links.along_y)])
        elif kind == "all_y":
            self.second = Stage(links, [(total.at[y, 1 - x], two, links.along_x)])
        if kind in ("all_x", "all_y"):
            self.line = LineSum(links, lambda at: total.at[y, x, at], three)

    def begin(self):
        self.core.start()

    def add(self, pairs, count):
        total = self.total

        def body(i, carry):
            index, extra = pairs(i)
            total[index] = total[index] + extra
            return carry

        lax.fori_loop(0, count, body, 0)

    def run_first(self):
        self.core.wait()
        sib = self.sib
        if self.kind == "down":
            self.add(lambda i: ((i // 4, i % 4), sib[i // 4, i % 4]), 8)
        else:
            self.add(lambda i: ((i // 8, i // 4 % 2, i % 4), sib[i // 8, i // 4 % 2, i % 4]), 16)
        self.first.start()

    def run_second(self):
        self.first.wait()
        one = self.one
        if self.kind == "down":
            self.add(lambda i: ((self.q, i), one[i]), 4)
        else:
            self.add(lambda i: (self.kept(i // 4, i % 4), one[i // 4, i % 4]), 8)
        if self.kind in ("all_x", "all_y"):
            self.second.start()
        else:
            self.line.start()

    def run_third(self):
        self.second.wait()
        y, x, two = self.links.y, self.links.x, self.two
        self.add(lambda i: ((y, x, i), two[i]), 4)
        self.line.start()

    def run_last(self):
        z, total, got = self.links.z, self.total, self.three

        def add(slot):
            for i in range(2):
                index = self.kept(i, z)
                total[index] = total[index] + got[slot, i]

        self.line.collect(add)
        self.last.start()

    def finish(self, out):
        y, x, z = self.links.y, self.links.x, self.links.z
        if self.kind in ("up_y", "up_x"):
            self.last.wait()
            along_x = self.kind == "up_y"
            mine = x if along_x else y
            for number, part in ((mine, self.total[y, x, z]), (1 - mine, self.two[...])):
                for j in range(8):
                    place = (j // 4 * 2 + number) if along_x else (number * 2 + j // 4)
                    start = (place * 4 + j % 4) * 256 + (0 if along_x else 128)
                    at = pl.ds(pl.multiple_of(start, 128), 128)
                    out[:, at] = part[:, j * 128 : (j + 1) * 128].astype(jnp.float32)
            return
        out[...] = (self.total[self.q, z] if self.kind == "down" else self.total[y, x, z]).astype(jnp.float32)

        def add(slot):
            out[...] = out[...] + self.three[slot].astype(jnp.float32)

        self.line.collect(add)


def front_kernel(scaling, *refs):
    live_ref, tokens, norm_gains, grad_masks, mask_norm = refs[:5]
    qkv_shard, out_shard, up_given, down_shard, patch_shard, class_shard = refs[5:11]
    attended, heads_ref, logsum, rows_ref, gains_ref, qkv, class_masks, mask_sums = refs[11:19]
    normal_one, inverse_one, normed_two, active, d_branch, d_hidden = refs[19:25]
    d_mix, d_second, d_attended, g_patch, g_class = refs[25:30]
    refs = refs[30:]
    full_out, ups, downs, full_patch, full_class, tiles, staged = refs[:7]
    slope, stream, normal_two, inverse_two, patch_proj, class_proj, classes = refs[7:14]
    part_sent, part_got, back_sent, back_got, class_sent, class_got = refs[14:20]
    term_sent, term_got, mask_in, tile, up_shard = refs[20:25]
    rounded, d_patch, class_rows, d_class = refs[25:29]
    patch_parts, class_parts = refs[29:34], refs[34:39]
    send_sem, recv_sem, local_sem = refs[39:]
    second = residual = d_residual = stream
    links = Links(send_sem, recv_sem)
    y, x, z, c = links.y, links.x, links.z, links.c
    h = y * 2 + x
    q = y * (1 - c) + x * c
    rows, features = tokens.shape
    wide = qkv.shape[-1]
    narrow = staged.shape[1]
    heads = narrow // DH
    block = ups.shape[-1]
    slot_rows = rows * 4
    plane = [(links.across, 3 - h, 3), (links.along_x, y * 2 + 1 - x, 1), (links.along_y, (1 - y) * 2 + x, 2)]
    at_x, at_y = plane[1][1], plane[2][1]

    def columns(start, size):
        return pl.ds(pl.multiple_of(start, 128), size)

    def up_block(number):
        return up_shard.at[:, columns(number * block, block)]

    local = [
        pltpu.make_async_copy(source, target, local_sem.at[number])
        for number, (source, target) in zip(
            (0, 1, 2, 3, 4, 5, 7, 8),
            [
                (tile, tiles.at[y, x, z, c]),
                (qkv_shard.at[:, columns(h * wide, wide)], qkv.at[y, x, z, c]),
                (out_shard, full_out.at[y, x, z, c]),
                (down_shard, downs.at[c, q, z]),
                (up_block(x), ups.at[0, y, x, z, c]),
                (up_block(2 + y), ups.at[1, y, x, z, c]),
                (patch_shard, full_patch.at[y, x, z, c]),
                (class_shard, full_class.at[y, x, z, c]),
            ]
        )
    ]
    gain_core = Stage(links, [(tile, tiles.at[y, x, z, c], links.sibling)])
    gain_z = Stage(links, [(tiles.at[y, x, z], tiles.at[y, x, z], peer) for peer in links.along_z])
    gain_plane = Stage(links, [(tiles.at[y, x], tiles.at[y, x], peer) for peer, _, _ in plane])
    qkv_plane = Stage(
        links, [(qkv_shard.at[:, columns(p * wide, wide)], qkv.at[y, x, z, c], peer) for peer, p, _ in plane]
    )
    part = qkv.shape[4] // 2
    qkv_z = [Line(links, lambda at, k=k: qkv.at[:, :, at, c, k * part : (k + 1) * part]) for k in range(2)]
    qkv_core = Stage(links, [(qkv.at[:, :, :, c], qkv.at[:, :, :, c], links.sibling)])
    up_split = [
        Stage(links, [(up_block(1 - x), ups.at[0, y, x, z, c], links.along_x)]),
        Stage(links, [(up_block(2 + 1 - y), ups.at[1, y, x, z, c], links.along_y)]),
    ]
    up_z = [
        Line(links, lambda at: ups.at[0, y, :, at, c]),
        Line(links, lambda at: ups.at[1, :, x, at, c]),
    ]
    up_on = [
        Stage(links, [(ups.at[0, y, :, :, c], ups.at[0, y, :, :, c], links.along_y)]),
        Stage(links, [(ups.at[1, :, x, :, c], ups.at[1, :, x, :, c], links.along_x)]),
    ]
    up_core = [
        Stage(links, [(ups.at[k, :, :, :, c], ups.at[k, :, :, :, c], links.sibling)]) for k in range(2)
    ]
    some = down_shard.shape[0] // 4
    turned = device(y + (1 - c) * (1 - 2 * y), x + c * (1 - 2 * x), z, c)
    spans = [slice(k * some, (k + 1) * some) for k in range(4)]
    down_turn = [Stage(links, [(down_shard.at[spans[k]], downs.at[c, q, z, spans[k]], turned)]) for k in (0, 1)]
    down_z = [Line(links, lambda at, k=k: downs.at[c, :, at, spans[k]]) for k in (0, 1)] + [
        Line(links, lambda at, k=k: downs.at[c, q, at, spans[k]], down_shard.at[spans[k]]) for k in (2, 3)
    ]
    down_on = [Stage(links, [(downs.at[c, q, :, spans[k]],) * 2 + (turned,)]) for k in (2, 3)]
    down_core = [
        Stage(links, [(downs.at[c, :, :, span], downs.at[c, :, :, span], links.sibling)])
        for span in (slice(0, 2 * some), slice(2 * some, 4 * some))
    ]
    patch_sum = Sum(links, *patch_parts, "all_x")
    class_sum = Sum(links, *class_parts, "all_y")
    part = out_shard.shape[0] // 2

    def square(full, shard):
        first = [full.at[y, x, :, c, 0:part], full.at[y, x, :, c, part:]]
        second = [full.at[:, x, :, c, 0:part], full.at[y, :, :, c, part:]]
        return (
            Line(links, lambda at: full.at[y, x, at, c], shard),
            Stage(links, [(first[0], first[0], links.along_y), (first[1], first[1], links.along_x)]),
            Stage(links, [(second[0], second[0], links.along_x), (second[1], second[1], links.along_y)]),
            Stage(links, [(full.at[:, :, :, c],) * 2 + (links.sibling,)]),
        )

    out_z, out_one, out_two, out_core = square(full_out, out_shard)
    near, far = slice(0, part), slice(part, 2 * part)
    patch_x = Stage(links, [(patch_shard.at[far], full_patch.at[y, x, z, c, far], links.along_x)])
    patch_y = Stage(links, [(full_patch.at[y, :, z, c, far],) * 2 + (links.along_y,)])
    patch_first = Line(links, lambda at: full_patch.at[y, x, at, c, near], patch_shard.at[near])
    patch_one = Stage(links, [(full_patch.at[y, x, :, c, near],) * 2 + (links.along_y,)])
    patch_two = Stage(links, [(full_patch.at[:, x, :, c, near],) * 2 + (links.along_x,)])
    class_y = Stage(links, [(class_shard, full_class.at[y, x, z, c], links.along_y)])
    class_x = Stage(links, [(full_class.at[:, x, z, c],) * 2 + (links.along_x,)])
    halves = [slice(k * part, (k + 1) * part) for k in range(2)]
    class_z = [Line(links, lambda at, k=k: full_class.at[:, :, at, c, k * part : (k + 1) * part]) for k in range(2)]
    halves = [slice(part + k * part // 2, part + (k + 1) * part // 2) for k in range(2)]
    patch_z = [Line(links, lambda at, k=k: full_patch.at[:, :, at, c, halves[k]]) for k in range(2)]
    patch_core = Stage(links, [(full_patch.at[:, :, :, c],) * 2 + (links.sibling,)])
    class_core = Stage(links, [(full_class.at[:, :, :, c],) * 2 + (links.sibling,)])
    beside = (links.along_x, links.along_y)
    here = slice(0, rows)
    few = class_proj.shape[0]
    tall = -(-CLS // 16) * 16
    parts = (slice(0, tall), slice(tall, rows))
    theirs = [slice(rows + at.start, rows + at.stop) for at in parts]

    def exchange(sent, got, sent_at, got_at):
        return [
            [Stage(links, [(sent.at[k, sent_at[i]], got.at[k, got_at[i]], beside[k])]) for i in range(2)]
            for k in range(2)
        ]

    normed_out = exchange(normed_two, normed_two, parts, theirs)
    branch_out = exchange(d_branch, d_branch, parts, theirs)
    part_back = exchange(part_sent, part_got, parts, parts)
    grad_back = exchange(back_sent, back_got, parts, parts)
    sizes = {1: few, 2: few, 3: tall - 3 * few}
    class_out = [
        links.plan(
            rounded.at[few * rel : few * rel + sizes[rel]], class_rows.at[0 : sizes[rel]], peer, h == 0
        )
        for peer, _, rel in plane
    ]
    mine = pl.ds(pl.multiple_of(h * few, few), few)
    unit_out = Stage(links, [(classes.at[mine], classes.at[mine], peer) for peer, _, _ in plane])
    class_back = Stage(links, [(class_sent.at[p], class_got.at[rel - 1], peer) for peer, p, rel in plane])
    term_back = [
        links.plan(term_sent.at[0 : sizes[rel]], term_got.at[rel - 1, 0 : sizes[rel]], peer, h == rel)
        for peer, _, rel in plane
    ]
    middle = rows // 2
    strips = [slice(0, middle), slice(middle, rows)]
    rows_x = [Stage(links, [(rows_ref.at[h, strips[k]],) * 2 + (links.along_x,)]) for k in (0, 1)]
    rows_y = [Stage(links, [(rows_ref.at[h, strips[k]],) * 2 + (links.along_y,)]) for k in (1, 0)]
    piece_a, piece_b = rows_ref.at[at_x, strips[0]], rows_ref.at[at_y, strips[1]]
    relay_y = Stage(links, [(piece_a, piece_a, links.along_y)])
    relay_x = Stage(links, [(piece_b, piece_b, links.along_x)])

    share = norm_gains.shape[1]
    tile[...] = jnp.zeros_like(tile)
    for i in range(4):

        @pl.when((z * 2 + c) % 4 == i)
        def _(i=i):
            tile[0:2, i * share : (i + 1) * share] = norm_gains[...].astype(jnp.float32)

    for number in range(4):
        for j in range(8):
            at = (j // 4 * 2 + number) if number < 2 else ((number - 2) * 2 + j // 4)
            at = (at * 4 + j % 4) * 256 + (0 if number < 2 else 128)
            up_shard[:, number * block + j * 128 : number * block + (j + 1) * 128] = up_given[:, at : at + 128]
    for copy in local:
        copy.start()
    class_rows[...] = jnp.zeros_like(class_rows)
    links.greet()
    for stage in (gain_core, qkv_plane, *up_split, *down_turn, class_y, patch_x, out_z, patch_first):
        stage.start()
    value, inverse = norm(tokens[...])
    normal_one[...] = value
    inverse_one[...] = jnp.broadcast_to(inverse, inverse_one.shape)
    local[0].wait()
    gain_core.wait()
    gain_z.start()
    gain_z.wait()
    gain_plane.start()
    local[1].wait()
    qkv_plane.wait()
    for line in qkv_z:
        line.start()
    gain_plane.wait()
    for j in range(8):
        piece = tiles[j // 4, j // 2 % 2, (j % 2) * 2, 0].astype(jnp.float32)
        for i in range(1, 4):
            piece = piece + tiles[j // 4, j // 2 % 2, (j % 2) * 2 + i // 2, i % 2].astype(jnp.float32)
        gains_ref[:, j * 128 : (j + 1) * 128] = piece[0:8]
    rows_ref[h] = (normal_one[...] * gains_ref[0:1, :]).astype(jnp.bfloat16)
    for stage in (rows_x[0], rows_y[0], rows_x[1], rows_y[1]):
        stage.start()
    for line in (out_z, patch_first, *qkv_z):
        line.relay()
    rows_x[0].wait()
    relay_y.start()
    rows_y[0].wait()
    relay_x.start()
    local[6].wait()
    patch_x.wait()
    patch_y.start()
    local[7].wait()
    class_y.wait()
    class_x.start()
    for line in qkv_z:
        line.wait()
    qkv_core.start()
    for k in range(2):
        local[4 + k].wait()
        up_split[k].wait()
        up_z[k].start()
    out_z.wait()
    patch_first.wait()
    for number in (2, 3):
        local[number].wait()

    def project(p):
        weight = qkv[...].reshape(rows * 4, wide)
        piece = jnp.dot(rows_ref[p], weight, preferred_element_type=jnp.float32).astype(jnp.bfloat16)
        at = pl.ds(pl.multiple_of(p * rows, rows), rows)
        for number in range(3 * heads):
            heads_ref[number, at, :] = piece[:, number * DH : (number + 1) * DH]

    qkv_core.wait()
    project(h)
    rows_x[1].wait()
    project(at_x)
    rows_y[1].wait()
    project(at_y)
    out_one.start()
    patch_one.start()
    relay_y.wait()
    relay_x.wait()
    project(3 - h)

    live = live_ref[0]
    key_live = lax.broadcasted_iota(jnp.int32, (slot_rows, 1), 0) < live
    returned = links.count - 1
    assert returned + 4 <= FRONT_COPIES

    def back(rel):
        peer = h + (rel % 2) * (1 - 2 * x) + (rel // 2) * (2 - 4 * y)
        return pltpu.make_async_remote_copy(
            src_ref=staged.at[pl.ds(pl.multiple_of(peer * rows, rows), rows), :],
            dst_ref=attended.at[:, columns(h * narrow, narrow)],
            send_sem=send_sem.at[returned + rel],
            recv_sem=recv_sem.at[returned + rel],
            device_id=(peer, z * 2 + c),
            device_id_type=MESH,
        )

    def up_next(k):
        up_z[k].wait()
        up_on[k].start()

    def up_end(k):
        up_on[k].wait()
        up_core[k].start()

    def out_next():
        out_one.wait()
        out_two.start()

    def out_end():
        out_two.wait()
        out_core.start()

    def patch_next():
        patch_one.wait()
        patch_two.start()

    def down_late():
        down_z[2].start()
        down_z[3].start()

    def down_early():
        for stage in down_turn:
            stage.wait()
        down_z[0].start()
        down_z[1].start()

    def down_relays():
        down_z[2].relay()
        down_z[3].relay()

    events = {
        0: up_z[0].relay,
        3: out_next,
        5: up_z[1].relay,
        6: down_late,
        11: down_early,
        12: out_end,
        14: down_relays,
    }

    def tile_body(slot, carry):
        turn, number = slot // 4, slot % 4
        rel = 3 - turn
        peer = h + (rel % 2) * (1 - 2 * x) + (rel // 2) * (2 - 4 * y)
        at = pl.ds(pl.multiple_of(peer * rows, rows), rows)
        at_slots(slot, events)
        queries = heads_ref[3 * number, at, :]
        keys = heads_ref[3 * number + 1]
        values = heads_ref[3 * number + 2]
        scores = lax.dot_general(keys, queries, (((1,), (1,)), ((), ())), preferred_element_type=jnp.float32)
        scores = jnp.where(key_live, scores * (scaling * LOG2E), -1e30)
        highest = jnp.max(scores, axis=0, keepdims=True)
        raw = jnp.exp2(scores - highest)
        totals = jnp.sum(raw, axis=0, keepdims=True)
        weights = (raw * (1.0 / totals)).astype(jnp.bfloat16)
        mixed = lax.dot_general(
            values, weights, (((0,), (0,)), ((), ())), preferred_element_type=jnp.float32
        )
        mixed = mixed.T.astype(jnp.bfloat16)
        for which in range(4):

            @pl.when(number == which)
            def _(which=which):
                staged[at, which * DH : (which + 1) * DH] = mixed

        logsum[number, :, at] = highest + jnp.log2(totals)

        @pl.when((number == 3) & (rel > 0))
        def _():
            back(rel).start()

        return carry

    lax.fori_loop(0, SLOTS, tile_body, 0)
    own = pltpu.make_async_copy(
        staged.at[pl.ds(pl.multiple_of(h * rows, rows), rows), :],
        attended.at[:, columns(h * narrow, narrow)],
        local_sem.at[6],
    )
    own.start()
    class_x.wait()
    patch_y.wait()
    for line in (*class_z, *patch_z):
        line.start()
    up_next(0)
    up_next(1)
    for k in range(2):
        down_z[2 + k].wait()
        down_on[k].start()
    for rel in (3, 2, 1):
        back(rel).wait()
    own.wait()
    out_core.wait()
    down_z[0].relay()

    def whole(weight):
        return weight[...].reshape(-1, weight.shape[-1])

    second[...] = tokens[...] + matmul(attended[...], whole(full_out))
    value, inverse = norm(second[...])
    normal_two[...] = value
    inverse_two[...] = jnp.broadcast_to(inverse, inverse_two.shape)
    value = (value * gains_ref[1:2, :]).astype(jnp.bfloat16)
    for k in range(2):
        normed_two[k, here] = value
    for i in range(2):
        for k in range(2):
            normed_out[k][i].start()
    down_z[1].relay()
    patch_next()
    up_end(0)
    up_end(1)
    for k in range(2):
        up_core[k].wait()
    wide_step = 256

    def forward(k, at, size):
        def step(j, carry):
            span = pl.ds(pl.multiple_of(j * wide_step, wide_step), wide_step)
            weight = ups[k, :, :, :, :, :, span].reshape(features, wide_step)
            hidden = matmul(normed_two[k, at], weight)
            spread = 0.5 + 0.5 * lax.erf(hidden * 0.7071067811865476)
            density = jnp.exp(hidden * hidden * -0.5) * 0.3989422804014327
            active[k, at, span] = (hidden * spread).astype(jnp.bfloat16)
            slope[k, at, span] = spread + hidden * density
            return carry

        lax.fori_loop(0, block // wide_step, step, 0)

    forward(0, here, rows)
    for stage in down_on:
        stage.wait()
    down_core[1].start()
    forward(1, here, rows)
    for line in down_z[:2]:
        line.wait()
    down_core[0].start()
    for stage in down_core:
        stage.wait()
    for i in range(2):
        for k in range(2):
            normed_out[k][i].wait()
            forward(k, theirs[i], parts[i].stop - parts[i].start)
            part_sent[k, parts[i]] = matmul(active[k, theirs[i]], whole(downs.at[k])).astype(jnp.bfloat16)
            part_back[k][i].start()
        if i == 0:
            for line in class_z:
                line.relay()
    residual[...] = second[...] + (
        matmul(active[0, here], whole(downs.at[0])) + matmul(active[1, here], whole(downs.at[1]))
    )
    for line in patch_z:
        line.relay()

    def complete(at):
        for k in range(2):
            part_back[k][0 if at.start == 0 else 1].wait()
        value = residual[at] + (part_got[0, at].astype(jnp.float32) + part_got[1, at].astype(jnp.float32))
        rounded[at] = value.astype(jnp.bfloat16)

    complete(parts[0])

    @pl.when(h == 0)
    def _():
        for copy in class_out:
            copy.start()
        class_rows[...] = rounded[0:few]

    for line in class_z:
        line.wait()
    class_core.start()
    complete(parts[1])
    for line in patch_z:
        line.wait()
    patch_two.wait()
    patch_core.start()
    patch_core.wait()

    patch_proj[...] = matmul(rounded[...], whole(full_patch))
    factor = unit_scale(patch_proj[...])
    patch_unit = (patch_proj[...] * factor).astype(jnp.bfloat16)
    classes[4 * few :] = jnp.zeros((classes.shape[0] - 4 * few, features), jnp.bfloat16)
    for copy, (_, _, rel) in zip(class_out, plane):
        pl.when(h == rel)(copy.wait_recv)
    class_core.wait()
    class_live = h * few + lax.broadcasted_iota(jnp.int32, (few, 1), 0) < CLS
    value = matmul(class_rows[...], whole(full_class))
    class_proj[...] = value
    classes[mine] = jnp.where(class_live, value * unit_scale(value), 0.0).astype(jnp.bfloat16)
    unit_out.start()
    mask_in[...] = jnp.zeros_like(mask_in)
    mask_in[0:rows, 0:CLS] = grad_masks[...]
    mask_in[rows : rows + 2, 0:CLS] = mask_norm[...]
    mask_gain, mask_bias = mask_in[rows : rows + 1, :], mask_in[rows + 1 : rows + 2, :]
    unit_out.wait()
    products = matmul_nt(patch_unit, classes[...])
    lane = lax.broadcasted_iota(jnp.int32, products.shape, 1)
    position = h * rows + lax.broadcasted_iota(jnp.int32, (rows, 1), 0)
    patch_rows = ((position >= CLS) & (position < live)).astype(jnp.float32)

    def class_mean(values):
        return jnp.sum(values, axis=-1, keepdims=True) * (1.0 / CLS)

    center = jnp.where(lane < CLS, products - class_mean(products), 0.0)
    inverse = lax.rsqrt(class_mean(center * center) + 1e-05)
    mask_normal = center * inverse
    class_masks[...] = ((mask_normal * mask_gain + mask_bias) * patch_rows)[:, 0:CLS]
    upstream = mask_in[0:rows, :] * patch_rows
    mask_sums[...] = jnp.zeros_like(mask_sums)
    mask_sums[0:1, :] = jnp.sum(upstream * mask_normal, axis=0, keepdims=True)
    mask_sums[1:2, :] = jnp.sum(upstream, axis=0, keepdims=True)
    upstream = upstream * mask_gain
    upstream = inverse * (upstream - class_mean(upstream) - mask_normal * class_mean(upstream * mask_normal))
    d_products = jnp.where(lane < CLS, upstream, 0.0).astype(jnp.bfloat16)
    class_part = matmul_tn(d_products, patch_unit)
    for p in range(4):
        class_sent[p] = class_part[few * p : few * (p + 1)].astype(jnp.bfloat16)
    class_back.start()
    upstream = matmul(d_products, classes[...])
    direct = patch_proj[...] * factor
    upstream = factor * (upstream - direct * jnp.sum(upstream * direct, axis=-1, keepdims=True))
    d_patch[...] = upstream.astype(jnp.bfloat16)
    d_residual[...] = matmul_nt(d_patch[...], whole(full_patch))

    def branch(i):
        value = d_residual[parts[i]].astype(jnp.bfloat16)
        for k in range(2):
            d_branch[k, parts[i]] = value
            branch_out[k][i].start()

    branch(1)

    weight_gradient(patch_parts[0], rounded, d_patch)
    patch_sum.begin()
    class_back.wait()
    upstream = class_sent[h].astype(jnp.float32)
    for number in range(3):
        upstream = upstream + class_got[number].astype(jnp.float32)
    d_class[...] = jnp.where(class_live, unit_back(class_proj[...], upstream), 0.0).astype(jnp.bfloat16)
    term = matmul_nt(d_class[...], whole(full_class))
    term_sent[...] = term.astype(jnp.bfloat16)
    for copy, (_, _, rel) in zip(term_back, plane):
        pl.when(h == rel)(copy.start)
    weight_gradient(class_parts[0], class_rows, d_class)
    class_sum.begin()

    def backward(k, at):
        for j in range(block // wide_step):
            weight = downs[k, j // 2, 2 * (j % 2) : 2 * (j % 2) + 2].reshape(wide_step, features)
            span = slice(j * wide_step, (j + 1) * wide_step)
            d_hidden[k, at, span] = (matmul_nt(d_branch[k, at], weight) * slope[k, at, span]).astype(jnp.bfloat16)


    def returned_rows(i):
        for k in range(2):
            branch_out[k][i].wait()
            backward(k, theirs[i])
            back_sent[k, parts[i]] = matmul_nt(d_hidden[k, theirs[i]], whole(ups.at[k])).astype(jnp.bfloat16)
            grad_back[k][i].start()

    for k in range(2):
        backward(k, parts[1])
    returned_rows(1)

    @pl.when(h == 0)
    def _():
        d_residual[0:few] = d_residual[0:few] + term_sent[...].astype(jnp.float32)
        for copy, (_, _, rel) in zip(term_back, plane):
            copy.wait_recv()
            at = slice(few * rel, few * rel + sizes[rel])
            d_residual[at] = d_residual[at] + term_got[rel - 1, 0 : sizes[rel]].astype(jnp.float32)

    branch(0)
    patch_sum.run_first()
    class_sum.run_first()
    for k in range(2):
        backward(k, parts[0])
    returned_rows(0)
    upstream = matmul_nt(d_hidden[0, here], whole(ups.at[0])) + matmul_nt(d_hidden[1, here], whole(ups.at[1]))
    patch_sum.run_second()
    class_sum.run_second()
    for k in range(2):
        for stage in grad_back[k]:
            stage.wait()
    upstream = upstream + (back_got[0].astype(jnp.float32) + back_got[1].astype(jnp.float32))
    upstream = upstream * gains_ref[1:2, :]
    value = normal_two[...]
    middle = jnp.mean(upstream, axis=-1, keepdims=True)
    along = jnp.mean(upstream * value, axis=-1, keepdims=True)
    d_second[...] = d_residual[...] + inverse_two[:, 0:1] * (upstream - middle - value * along)
    patch_sum.run_third()
    class_sum.run_third()
    d_mix[...] = d_second[...].astype(jnp.bfloat16)
    d_attended[...] = matmul_nt(d_mix[...], whole(full_out)).astype(jnp.bfloat16)
    patch_sum.line.relay()
    class_sum.line.relay()
    patch_sum.finish(g_patch)
    class_sum.finish(g_class)
    links.drain()


def front(live, tokens, norm_gains, grad_masks, mask_norm, shards, scaling):
    rows, features = tokens.shape
    vmem, hbm = pl.BlockSpec(memory_space=pltpu.VMEM), pl.BlockSpec(memory_space=pl.ANY)
    w_qkv, w_out, w_up, w_down, w_patch, w_class = shards
    wide = w_qkv.shape[1] // 4
    heads = wide // (3 * DH)
    block = w_up.shape[1] // 4
    lanes = 256
    few = -(-CLS // 64) * 16
    low, single = jnp.bfloat16, jnp.float32
    outs = [
        ((rows, features), low),
        ((3 * heads, 4 * rows, DH), low),
        ((heads, 1, 4 * rows), single),
        ((4, rows, features), low),
        ((8, features), single),
        ((2, 2, 4, 2, w_qkv.shape[0], wide), low),
        (grad_masks.shape, single),
        ((8, lanes), single),
        ((rows, features), single),
        ((rows, 128), single),
        ((2, 2 * rows, features), low),
        ((2, 2 * rows, block), low),
        ((2, 2 * rows, features), low),
        ((2, 2 * rows, block), low),
        ((rows, features), low),
        ((rows, features), single),
        ((rows, features), low),
        (w_patch.shape, single),
        (w_class.shape, single),
    ]
    scratch = [
        ((2, 2, 4, 2) + w_out.shape, low),
        ((2, 2, 2, 4, 2, w_up.shape[0], block), low),
        ((2, 2, 4) + w_down.shape, low),
        ((2, 2, 4, 2) + w_patch.shape, low),
        ((2, 2, 4, 2) + w_class.shape, low),
        ((2, 2, 4, 2, 8, 128), single),
        ((4 * rows, wide // 3), low),
        ((2, 2 * rows, block), single),
        ((rows, features), single),
        ((rows, features), single),
        ((rows, 128), single),
        ((rows, features), single),
        ((few, features), single),
        ((lanes, features), low),
        ((2, rows, features), low),
        ((2, rows, features), low),
        ((2, rows, features), low),
        ((2, rows, features), low),
        ((4, few, features), low),
        ((3, few, features), low),
        ((few, features), low),
        ((3, few, features), low),
        ((rows + 8, lanes), single),
        ((8, 128), single),
        (w_up.shape, low),
        ((rows, features), low),
        ((rows, features), low),
        ((few, features), low),
        ((few, features), low),
    ]
    for shape in (w_patch.shape, w_class.shape):
        for lead in ((2, 2, 4, 2), (2, 2, 4), (2, 4), (4,), (5,)):
            scratch.append((lead + shape, low))
    return pl.pallas_call(
        partial(front_kernel, scaling),
        out_shape=[jax.ShapeDtypeStruct(*out) for out in outs],
        in_specs=[pl.BlockSpec(memory_space=pltpu.SMEM)] + [vmem] * 4 + [hbm] * 2 + [vmem] + [hbm] * 3,
        out_specs=[vmem] * len(outs),
        scratch_shapes=[pltpu.VMEM(*shape) for shape in scratch]
        + [
            pltpu.SemaphoreType.DMA((FRONT_COPIES,)),
            pltpu.SemaphoreType.DMA((FRONT_COPIES,)),
            pltpu.SemaphoreType.DMA((9,)),
        ],
        compiler_params=pltpu.CompilerParams(
            collective_id=1, has_side_effects=True, vmem_limit_bytes=121 * 2**19
        ),
        name="front",
    )(live, tokens, norm_gains, grad_masks, mask_norm, *shards)


def rear_kernel(scaling, *refs):
    live_ref, d_rows, heads_ref, logsum, rows_ref, qkv, small_ref = refs[:7]
    normal_one, inverse_one, d_second, gains_ref = refs[7:11]
    refs = refs[:7] + refs[11:]
    normed_two, active, d_branch, d_hidden, attended, d_mix = refs[7:13]
    d_normed, g_qkv, g_up, g_down, g_out, small_out = refs[13:19]
    at = 19
    d_out, d_heads, d_spread, grad_keys, grad_values = refs[at : at + 5]
    d_sent, d_got, q_part, q_sib, q_z, q_plane = refs[at + 5 : at + 11]
    small_own, small_got, send_sem, recv_sem, local_sem = refs[at + 11 : at + 16]
    scratch = refs[at + 16 :]
    links = Links(send_sem, recv_sem)
    y, x, z, c = links.y, links.x, links.z, links.c
    h = y * 2 + x
    rows, features = d_rows.shape
    slot_rows = rows * 4
    narrow = d_out.shape[1]
    heads = narrow // DH
    wide = 3 * narrow
    plane = [(links.across, 3 - h, 3), (links.along_x, y * 2 + 1 - x, 1), (links.along_y, (1 - y) * 2 + x, 2)]

    def columns(start, size):
        return pl.ds(pl.multiple_of(start, 128), size)

    def block(p):
        return pl.ds(pl.multiple_of(p * rows, rows), rows)

    spread_out = Stage(
        links, [(d_rows.at[:, columns(p * narrow, narrow)], d_out.at[block(h), :], peer) for peer, p, _ in plane]
    )
    own = pltpu.make_async_copy(d_rows.at[:, columns(h * narrow, narrow)], d_out.at[block(h), :], local_sem.at[0])
    kinds = ("up_y", "up_x", "down", "all_x")
    sums = [
        Sum(links, *scratch[5 * i : 5 * i + 5], kinds[i]) for i in range(4)
    ]
    back = [Stage(links, [(d_sent.at[rel - 1], d_got.at[rel - 1], peer)]) for peer, _, rel in plane]
    q_core = Stage(links, [(q_part.at[:, :, :, 1 - c], q_sib, links.sibling)])
    q_line = LineSum(links, lambda at: q_part.at[:, :, at, c], q_z)
    q_across = Stage(
        links, [(q_part.at[p // 2, p % 2, z, c], q_plane.at[h], peer) for peer, p, _ in plane]
    )
    small_core = Stage(links, [(small_own.at[0], small_got.at[0], links.sibling)])
    small_x = Stage(links, [(small_own.at[1], small_got.at[1], links.along_x)])
    small_y = Stage(links, [(small_own.at[2], small_got.at[2], links.along_y)])
    small_z = Stage(links, [(small_own.at[3], small_got.at[3 + z], peer) for peer in links.along_z])

    links.greet()
    spread_out.start()
    own.start()
    small_own[0] = small_ref[...]
    small_core.start()
    parts = [scratch[5 * i] for i in range(4)]
    for k in range(2):
        weight_gradient(parts[k], normed_two.at[k], d_hidden.at[k])
        sums[k].begin()
    for k in range(2):
        weight_gradient(parts[2].at[k], active.at[k], d_branch.at[k])
    sums[2].begin()
    weight_gradient(parts[3], attended, d_mix)
    sums[3].begin()
    own.wait()
    spread_out.wait()
    live = live_ref[0]
    key_live = lax.broadcasted_iota(jnp.int32, (slot_rows, 1), 0) < live
    up_y, up_x, down, out = sums
    assert links.count <= REAR_COPIES

    def small_step(stage, number, following):
        def run():
            stage.wait()
            small_own[number + 1] = small_own[number] + small_got[number]
            if number == 2:
                small_got[3 + z] = small_own[3]
            following.start()

        return run

    def both(*steps):
        def run():
            for step in steps:
                step()

        return run

    events = {
        0: up_y.run_first,
        1: up_x.run_first,
        2: down.run_first,
        3: small_step(small_core, 0, small_x),
        6: out.run_first,
        7: small_step(small_x, 1, small_y),
        8: both(up_y.run_second, up_x.run_second),
        9: small_step(small_y, 2, small_z),
        11: both(up_y.line.relay, up_x.line.relay),
        13: down.run_second,
        15: both(up_y.run_last, up_x.run_last),
    }

    def tile_body(slot, carry):
        number, turn = slot // 4, slot % 4
        at_slots(slot, events)
        at = block(turn)

        @pl.when(turn == 0)
        def _():
            grad_keys[...] = jnp.zeros_like(grad_keys)
            grad_values[...] = jnp.zeros_like(grad_values)

        queries = heads_ref[3 * number, at, :]
        keys = heads_ref[3 * number + 1]
        values = heads_ref[3 * number + 2]
        grads = d_heads[number, at, :]
        scores = lax.dot_general(keys, queries, (((1,), (1,)), ((), ())), preferred_element_type=jnp.float32)
        powers = scores * (scaling * LOG2E) - logsum[number, :, at]
        weights = jnp.where(key_live, jnp.exp2(powers), 0.0)
        grad_values[...] += jnp.dot(weights.astype(jnp.bfloat16), grads, preferred_element_type=jnp.float32)
        grad_weights = lax.dot_general(
            values, grads, (((1,), (1,)), ((), ())), preferred_element_type=jnp.float32
        )
        deltas = jnp.sum(grad_weights * weights, axis=0, keepdims=True)
        grad_scores = (weights * (grad_weights - deltas)).astype(jnp.bfloat16)
        grad_keys[...] += jnp.dot(grad_scores, queries, preferred_element_type=jnp.float32)
        grad_queries = lax.dot_general(
            keys, grad_scores, (((0,), (0,)), ((), ())), preferred_element_type=jnp.float32
        )
        d_heads[4 + 3 * number, at, :] = (grad_queries.T * scaling).astype(jnp.bfloat16)

        @pl.when(turn == 3)
        def _():
            d_heads[5 + 3 * number] = (grad_keys[...] * scaling).astype(jnp.bfloat16)
            d_heads[6 + 3 * number] = grad_values[...].astype(jnp.bfloat16)

        return carry

    for number in range(heads):
        d_heads[number] = d_out[:, number * DH : (number + 1) * DH]
    lax.fori_loop(0, SLOTS, tile_body, 0)
    for number in range(3 * heads):
        d_spread[:, number * DH : (number + 1) * DH] = d_heads[4 + number]
    per = features // 4
    for j in range(4):
        left = jnp.concatenate([rows_ref[p, :, j * per : (j + 1) * per] for p in range(4)], axis=0)
        piece = lax.dot_general(
            left, d_spread[...], (((0,), (0,)), ((), ())), preferred_element_type=jnp.float32
        ).astype(jnp.bfloat16)
        q_part[j // 2, j % 2] = piece.reshape(4, 2, per // 8, wide)
    q_core.start()
    weight = qkv[...].reshape(features, wide)
    for (_, p, rel), stage in zip(plane, back):
        piece = lax.dot_general(
            d_spread[block(p), :], weight, (((1,), (1,)), ((), ())), preferred_element_type=jnp.float32
        )
        d_sent[rel - 1] = piece.astype(jnp.bfloat16)
        stage.start()
    q_core.wait()

    def add_sib(i, carry):
        index = (i // 8, i // 4 % 2, i % 4)
        q_part[(*index, c)] = q_part[(*index, c)] + q_sib[index]
        return carry

    lax.fori_loop(0, 16, add_sib, 0)
    q_line.start()
    d_normed[...] = lax.dot_general(
        d_spread[block(h), :], weight, (((1,), (1,)), ((), ())), preferred_element_type=jnp.float32
    )
    down.line.relay()
    q_line.relay()
    out.run_second()
    out.run_third()

    def add_line(slot):
        for i in range(4):
            index = (i // 2, i % 2)
            q_part[(*index, z, c)] = q_part[(*index, z, c)] + q_z[(slot, *index)]

    q_line.collect(add_line)
    q_across.start()
    out.line.relay()
    small_z.wait()
    small_out[...] = (small_got[3] + small_got[4] + small_got[5] + small_got[6])[0:2, 0:CLS]
    down.finish(g_down)
    up_y.finish(g_up)
    up_x.finish(g_up)
    out.finish(g_out)
    q_across.wait()
    g_qkv[:, columns(h * wide, wide)] = q_part[y, x, z, c].astype(jnp.float32)
    for _, p, _ in plane:
        g_qkv[:, columns(p * wide, wide)] = q_plane[p].astype(jnp.float32)
    for stage in back:
        stage.wait()
    upstream = d_normed[...] + (
        d_got[0].astype(jnp.float32) + d_got[1].astype(jnp.float32) + d_got[2].astype(jnp.float32)
    )
    upstream = upstream * gains_ref[0:1, :]
    value = normal_one[...]
    middle = jnp.mean(upstream, axis=-1, keepdims=True)
    along = jnp.mean(upstream * value, axis=-1, keepdims=True)
    d_normed[...] = d_second[...] + inverse_one[:, 0:1] * (upstream - middle - value * along)
    links.drain()


def rear(live, d_rows, heads_qkv, logsum, rows_all, qkv, small, ending, factors, scaling):
    rows, features = d_rows.shape
    slot_rows = 4 * rows
    narrow = features // 4
    heads = narrow // DH
    wide = 3 * narrow
    vmem, hbm = pl.BlockSpec(memory_space=pltpu.VMEM), pl.BlockSpec(memory_space=pl.ANY)
    low = jnp.bfloat16
    up, down = (features // 32, features), (features // 8, features)
    shard = (features // 32, wide)
    buffers = []
    for _ in range(2):
        buffers += [(2, 2, 4, 2) + up, (2, 2, 4) + up, (2, 4) + up, up, (5, 2) + up]
    buffers += [(2, 2, 4) + down, (2, 4) + down, (4,) + down, (8, 128), (5,) + down]
    buffers += [(2, 2, 4, 2) + up, (2, 2, 4) + up, (2, 4) + up, (4,) + up, (5,) + up]
    single = jnp.float32
    return pl.pallas_call(
        partial(rear_kernel, scaling),
        out_shape=[
            jax.ShapeDtypeStruct((rows, features), single),
            jax.ShapeDtypeStruct((features // 32, 4 * wide), single),
            jax.ShapeDtypeStruct((up[0], 4 * up[1]), single),
            jax.ShapeDtypeStruct(down, single),
        ]
        + [jax.ShapeDtypeStruct(up, single)]
        + [jax.ShapeDtypeStruct((2, CLS), single)],
        in_specs=[pl.BlockSpec(memory_space=pltpu.SMEM)] + [vmem] * 16,
        out_specs=[vmem] * 6,
        scratch_shapes=[
            pltpu.VMEM((slot_rows, narrow), low),
            pltpu.VMEM((4 * heads, slot_rows, DH), low),
            pltpu.VMEM((slot_rows, wide), low),
            pltpu.VMEM((slot_rows, DH), single),
            pltpu.VMEM((slot_rows, DH), single),
            pltpu.VMEM((3, rows, features), low),
            pltpu.VMEM((3, rows, features), low),
            pltpu.VMEM((2, 2, 4, 2) + shard, low),
            pltpu.VMEM((2, 2, 4) + shard, low),
            pltpu.VMEM((5, 2, 2) + shard, low),
            pltpu.VMEM((4,) + shard, low),
            pltpu.VMEM((4,) + small.shape, single),
            pltpu.VMEM((7,) + small.shape, single),
            pltpu.SemaphoreType.DMA((REAR_COPIES,)),
            pltpu.SemaphoreType.DMA((REAR_COPIES,)),
            pltpu.SemaphoreType.DMA((7,)),
        ]
        + [pltpu.VMEM(shape, low) for shape in buffers],
        compiler_params=pltpu.CompilerParams(
            collective_id=2, has_side_effects=True, vmem_limit_bytes=121 * 2**19
        ),
        name="rear",
    )(live, d_rows, heads_qkv, logsum, rows_all, qkv, small, *ending, *factors)


def ending_kernel(*refs):
    count = (len(refs) - 6) // 2
    results, (w_qkv, w_up, gains) = refs[:count], refs[count : count + 3]
    outs, gain_out, gain_sums, sems = refs[count + 3 : 2 * count + 3], *refs[2 * count + 3 :]
    copies = [pltpu.make_async_copy(results[i], outs[i], sems.at[i]) for i in range(count)]
    for copy in copies:
        copy.start()
    for number, (weight, grad) in enumerate(((w_qkv, results[2]), (w_up, results[4]))):
        total = jnp.sum(weight[...].astype(jnp.float32) * grad[...], axis=1, keepdims=True)
        total = jnp.broadcast_to(total, (total.shape[0], 128)).T[0:1, :]
        gain_sums[number : number + 1, :] = total / gains[number : number + 1, :].astype(jnp.float32)
    last = pltpu.make_async_copy(gain_sums, gain_out, sems.at[count])
    last.start()
    for copy in copies:
        copy.wait()
    last.wait()


def ending_copies(results, w_qkv, w_up, gains):
    vmem, hbm = pl.BlockSpec(memory_space=pltpu.VMEM), pl.BlockSpec(memory_space=pl.ANY)
    count = len(results)
    shapes = [jax.ShapeDtypeStruct(a.shape, a.dtype) for a in results]
    return pl.pallas_call(
        ending_kernel,
        out_shape=shapes + [jax.ShapeDtypeStruct(gains.shape, jnp.float32)],
        in_specs=[vmem] * (count + 3),
        out_specs=[hbm] * (count + 1),
        scratch_shapes=[pltpu.VMEM(gains.shape, jnp.float32), pltpu.SemaphoreType.DMA((count + 1,))],
        name="ending",
    )(*results, w_qkv, w_up, gains)


def body_planned(
    tokens,
    patch_counts,
    w_qkv,
    w_out,
    w_up,
    w_down,
    w_patch,
    w_class,
    norm_gains,
    mask_norm,
    grad_masks,
):
    low = jnp.bfloat16
    h, s = lax.axis_index("head"), lax.axis_index("seq")
    tokens, grad_masks = tokens[0], grad_masks[0]
    row_count = tokens.shape[0]
    live = CLS + patch_counts
    scaling = DH ** (-0.5)

    outs = front(
        live,
        tokens,
        norm_gains,
        grad_masks,
        mask_norm,
        (w_qkv, w_out, w_up, w_down, w_patch, w_class),
        scaling,
    )
    attended, heads_qkv, logsum, rows_all, gains, qkv, class_masks, mask_sums = outs[:8]
    normal_one, inverse_one, normed_two, active, d_branch, d_hidden = outs[8:14]
    d_mix, d_second, d_attended, g_patch, g_class = outs[14:]
    factors = (normed_two, active, d_branch, d_hidden, attended, d_mix)
    ending = (normal_one, inverse_one, d_second, gains)
    grad_inputs, g_qkv, g_up, g_down, g_out, sums = rear(
        live, d_attended, heads_qkv, logsum, rows_all, qkv, mask_sums, ending, factors, scaling
    )
    results = ending_copies(
        (class_masks, grad_inputs, g_qkv, g_out, g_up, g_down, g_patch, g_class, sums), w_qkv, w_up, norm_gains
    )
    return (results[0][None], results[1][None], *results[2:8], results[9], results[8])


def solution(mesh):
    planned = dict(mesh.shape) == {"head": 4, "seq": 8}
    return jax.shard_map(
        body_planned if planned else body_general,
        mesh=mesh,
        in_specs=(
            P("seq", "head", None),
            P("seq"),
            P(("head", "seq"), None),
            P(("head", "seq"), None),
            P(("head", "seq"), None),
            P(("head", "seq"), None),
            P(("head", "seq"), None),
            P(("head", "seq"), None),
            P(None, ("head", "seq")),
            P(),
            P("seq", "head", None),
        ),
        out_specs=(
            P("seq", "head", None),
            P("seq", "head", None),
            P(("head", "seq"), None),
            P(("head", "seq"), None),
            P(("head", "seq"), None),
            P(("head", "seq"), None),
            P(("head", "seq"), None),
            P(("head", "seq"), None),
            P(None, ("head", "seq")),
            P(),
        ),
        check_vma=False,
    )
```

profile of v0, /device:TPU:0, one launch (start us, length us, event | category | flops | bytes accessed | tf_op | source)
XLA Modules:
  0.0 292.0 jit_solution(7503486614077848085)
XLA Ops:
  1.3 1.8 copy.21
  3.0 180.2 %front.1 = (bf16[256,1024]{1,0:T(8,128)(2,1)}, bf16[12,1024,64]{2,1,0:T(8,128)(2,1)}, f32[4,1,1024]{2,1,0:T(1,128)}, bf16[4,256,1024]{2,1,0:T(8,128)(2,1)}, f32[...) custom-call(s32[1]{0:T(128)S(6)} %add.3.refs_0_, ...), custom_call_target="tpu_custom_call" | custom-call | tf_op jit(solution)/shard_map/front/pallas_call | solution.py:1254
  183.3 103.3 %rear.1 = (f32[256,1024]{1,0:T(8,128)}, f32[32,3072]{1,0:T(8,128)}, f32[32,4096]{1,0:T(8,128)}, f32[128,1024]{1,0:T(8,128)}, f32[32,1024]{1,0:T(8,128)}, /*index=5*/f32[2,150]{1,0:T(2,128)}) custom-call(s32[1]{0:T(128)S(6)} %add.3.refs_0_, bf16[256,1024]{1,0:T(8,128)(2,1)} %get-tuple-element.46.refs_1_, bf16[12,1024,64]{2,1,0:T(8,128)(2,1)} %get-tuple-element.47.refs_2_, ...), custom_call_target="tpu_custom_call" | custom-call | tf_op jit(solution)/shard_map/rear/pallas_call | solution.py:1490
  286.5 3.7 %ending.1 = (f32[256,150]{1,0:T(8,128)}, f32[256,1024]{1,0:T(8,128)}, f32[32,3072]{1,0:T(8,128)}, f32[32,1024]{1,0:T(8,128)}, f32[32,4096]{1,0:T(8,128)}, /*inde...) custom-call(f32[256,150]{1,0:T(8,128)} %get-tuple-element.45.refs_0_, ...), custom_call_target="tpu_custom_call" | custom-call | tf_op jit(solution)/shard_map/ending/pallas_call | solution.py:1550
  290.3 1.7 copy.22
where the time goes:
time: 292 us
  Pallas kernels  287 us (98%)
  local copies, waits for them, and re-layouts  3.48 us (1%)
    pallas_call x1, Pallas kernels, front(): pl.pallas_call(partial(front_kernel, scaling), out_shape=[jax.ShapeDtypeS...  180 us
    pallas_call x1, Pallas kernels, rear(): pl.pallas_call(partial(rear_kernel, scaling), out_shape=[jax.ShapeDtypeSt...  103 us

commit v1 on v0

--- a/solution.py
+++ b/solution.py
@@ -462,7 +462,7 @@
     def __init__(self, links, piece, got):
         self.links, self.piece, self.got = links, piece, got
         self.base = links.count
-        links.count += 5
+        links.count += 4
         links.lines.append(self)
 
     def copy(self, piece, target, slot, sent):
@@ -482,7 +482,7 @@
 
             @pl.when(z == end)
             def _(target=target, middle=middle):
-                self.copy(target, middle, 4, target).start()
+                self.copy(target, middle, middle, target).start()
 
         for target in range(4):
             direct = z != target
@@ -499,9 +499,9 @@
 
             @pl.when(z == middle)
             def _(target=target, middle=middle):
-                self.copy(target, target, 4, target).wait_recv()
+                self.copy(target, target, middle, target).wait_recv()
                 own = self.piece(target)
-                own[...] = own[...] + self.got[4]
+                own[...] = own[...] + self.got[middle]
                 self.copy(target, target, middle, target).start()
 
     def collect(self, add):
@@ -553,7 +553,7 @@
             self.second = Stage(links, [(total.at[1 - y, x], two, links.along_y)])
         elif kind == "all_y":
             self.second = Stage(links, [(total.at[y, 1 - x], two, links.along_x)])
-        if kind in ("all_x", "all_y"):
+        if kind in ("all_x", "all_y") and three is not None:
             self.line = LineSum(links, lambda at: total.at[y, x, at], three)
 
     def begin(self):
@@ -595,6 +595,12 @@
         y, x, two = self.links.y, self.links.x, self.two
         self.add(lambda i: ((y, x, i), two[i]), 4)
         self.line.start()
+
+    def hand_over(self, out):
+        self.second.wait()
+        y, x = self.links.y, self.links.x
+        for i in range(4):
+            out[i] = self.total[y, x, i] + self.two[i]
 
     def run_last(self):
         z, total, got = self.links.z, self.total, self.three
@@ -640,8 +646,8 @@
     part_sent, part_got, back_sent, back_got, class_sent, class_got = refs[14:20]
     term_sent, term_got, mask_in, tile, up_shard = refs[20:25]
     rounded, d_patch, class_rows, d_class = refs[25:29]
-    patch_parts, class_parts = refs[29:34], refs[34:39]
-    send_sem, recv_sem, local_sem = refs[39:]
+    patch_parts, class_parts = refs[29:33], refs[33:37]
+    send_sem, recv_sem, local_sem = refs[37:]
     second = residual = d_residual = stream
     links = Links(send_sem, recv_sem)
     y, x, z, c = links.y, links.x, links.z, links.c
@@ -714,8 +720,8 @@
         Stage(links, [(downs.at[c, :, :, span], downs.at[c, :, :, span], links.sibling)])
         for span in (slice(0, 2 * some), slice(2 * some, 4 * some))
     ]
-    patch_sum = Sum(links, *patch_parts, "all_x")
-    class_sum = Sum(links, *class_parts, "all_y")
+    patch_sum = Sum(links, *patch_parts, None, "all_x")
+    class_sum = Sum(links, *class_parts, None, "all_y")
     part = out_shard.shape[0] // 2
 
     def square(full, shard):
@@ -1175,14 +1181,10 @@
     middle = jnp.mean(upstream, axis=-1, keepdims=True)
     along = jnp.mean(upstream * value, axis=-1, keepdims=True)
     d_second[...] = d_residual[...] + inverse_two[:, 0:1] * (upstream - middle - value * along)
-    patch_sum.run_third()
-    class_sum.run_third()
     d_mix[...] = d_second[...].astype(jnp.bfloat16)
     d_attended[...] = matmul_nt(d_mix[...], whole(full_out)).astype(jnp.bfloat16)
-    patch_sum.line.relay()
-    class_sum.line.relay()
-    patch_sum.finish(g_patch)
-    class_sum.finish(g_class)
+    patch_sum.hand_over(g_patch)
+    class_sum.hand_over(g_class)
     links.drain()
 
 
@@ -1214,8 +1216,8 @@
         ((rows, features), low),
         ((rows, features), single),
         ((rows, features), low),
-        (w_patch.shape, single),
-        (w_class.shape, single),
+        ((4,) + w_patch.shape, low),
+        ((4,) + w_class.shape, low),
     ]
     scratch = [
         ((2, 2, 4, 2) + w_out.shape, low),
@@ -1249,7 +1251,7 @@
         ((few, features), low),
     ]
     for shape in (w_patch.shape, w_class.shape):
-        for lead in ((2, 2, 4, 2), (2, 2, 4), (2, 4), (4,), (5,)):
+        for lead in ((2, 2, 4, 2), (2, 2, 4), (2, 4), (4,)):
             scratch.append((lead + shape, low))
     return pl.pallas_call(
         partial(front_kernel, scaling),
@@ -1274,12 +1276,14 @@
     normal_one, inverse_one, d_second, gains_ref = refs[7:11]
     refs = refs[:7] + refs[11:]
     normed_two, active, d_branch, d_hidden, attended, d_mix = refs[7:13]
-    d_normed, g_qkv, g_up, g_down, g_out, small_out = refs[13:19]
-    at = 19
+    handed = refs[13:15]
+    d_normed, g_qkv, g_up, g_down, g_out, small_out, *g_handed = refs[15:23]
+    at = 23
     d_out, d_heads, d_spread, grad_keys, grad_values = refs[at : at + 5]
     d_sent, d_got, q_part, q_sib, q_z, q_plane = refs[at + 5 : at + 11]
     small_own, small_got, send_sem, recv_sem, local_sem = refs[at + 11 : at + 16]
-    scratch = refs[at + 16 :]
+    handed_own, handed_got = refs[at + 16 : at + 18]
+    scratch = refs[at + 18 :]
     links = Links(send_sem, recv_sem)
     y, x, z, c = links.y, links.x, links.z, links.c
     h = y * 2 + x
@@ -1315,11 +1319,16 @@
     small_y = Stage(links, [(small_own.at[2], small_got.at[2], links.along_y)])
     small_z = Stage(links, [(small_own.at[3], small_got.at[3 + z], peer) for peer in links.along_z])
 
+    handed_z = [LineSum(links, lambda at, k=k: handed_own.at[k, at], handed_got.at[k]) for k in range(2)]
+    for k in range(2):
+        handed_own[k] = handed[k][...]
     links.greet()
     spread_out.start()
     own.start()
     small_own[0] = small_ref[...]
     small_core.start()
+    for line in handed_z:
+        line.start()
     parts = [scratch[5 * i] for i in range(4)]
     for k in range(2):
         weight_gradient(parts[k], normed_two.at[k], d_hidden.at[k])
@@ -1353,18 +1362,28 @@
 
         return run
 
+    def handed_end():
+        for k in range(2):
+            out_ref = g_handed[k]
+            out_ref[...] = handed_own[k, z].astype(jnp.float32)
+
+            def add(slot, k=k, out_ref=out_ref):
+                out_ref[...] = out_ref[...] + handed_got[k, slot].astype(jnp.float32)
+
+            handed_z[k].collect(add)
+
     events = {
-        0: up_y.run_first,
+        0: both(handed_z[0].relay, handed_z[1].relay, up_y.run_first),
         1: up_x.run_first,
         2: down.run_first,
         3: small_step(small_core, 0, small_x),
+        5: handed_end,
         6: out.run_first,
         7: small_step(small_x, 1, small_y),
-        8: both(up_y.run_second, up_x.run_second),
-        9: small_step(small_y, 2, small_z),
-        11: both(up_y.line.relay, up_x.line.relay),
-        13: down.run_second,
-        15: both(up_y.run_last, up_x.run_last),
+        10: both(up_y.run_second, up_x.run_second),
+        11: small_step(small_y, 2, small_z),
+        13: both(up_y.line.relay, up_x.line.relay),
+        14: down.run_second,
     }
 
     def tile_body(slot, carry):
@@ -1423,6 +1442,8 @@
         )
         d_sent[rel - 1] = piece.astype(jnp.bfloat16)
         stage.start()
+    up_y.run_last()
+    up_x.run_last()
     q_core.wait()
 
     def add_sib(i, carry):
@@ -1483,9 +1504,9 @@
     shard = (features // 32, wide)
     buffers = []
     for _ in range(2):
-        buffers += [(2, 2, 4, 2) + up, (2, 2, 4) + up, (2, 4) + up, up, (5, 2) + up]
-    buffers += [(2, 2, 4) + down, (2, 4) + down, (4,) + down, (8, 128), (5,) + down]
-    buffers += [(2, 2, 4, 2) + up, (2, 2, 4) + up, (2, 4) + up, (4,) + up, (5,) + up]
+        buffers += [(2, 2, 4, 2) + up, (2, 2, 4) + up, (2, 4) + up, up, (4, 2) + up]
+    buffers += [(2, 2, 4) + down, (2, 4) + down, (4,) + down, (8, 128), (4,) + down]
+    buffers += [(2, 2, 4, 2) + up, (2, 2, 4) + up, (2, 4) + up, (4,) + up, (4,) + up]
     single = jnp.float32
     return pl.pallas_call(
         partial(rear_kernel, scaling),
@@ -1496,9 +1517,10 @@
             jax.ShapeDtypeStruct(down, single),
         ]
         + [jax.ShapeDtypeStruct(up, single)]
-        + [jax.ShapeDtypeStruct((2, CLS), single)],
-        in_specs=[pl.BlockSpec(memory_space=pltpu.SMEM)] + [vmem] * 16,
-        out_specs=[vmem] * 6,
+        + [jax.ShapeDtypeStruct((2, CLS), single)]
+        + [jax.ShapeDtypeStruct(up, single)] * 2,
+        in_specs=[pl.BlockSpec(memory_space=pltpu.SMEM)] + [vmem] * 18,
+        out_specs=[vmem] * 8,
         scratch_shapes=[
             pltpu.VMEM((slot_rows, narrow), low),
             pltpu.VMEM((4 * heads, slot_rows, DH), low),
@@ -1509,7 +1531,7 @@
             pltpu.VMEM((3, rows, features), low),
             pltpu.VMEM((2, 2, 4, 2) + shard, low),
             pltpu.VMEM((2, 2, 4) + shard, low),
-            pltpu.VMEM((5, 2, 2) + shard, low),
+            pltpu.VMEM((4, 2, 2) + shard, low),
             pltpu.VMEM((4,) + shard, low),
             pltpu.VMEM((4,) + small.shape, single),
             pltpu.VMEM((7,) + small.shape, single),
@@ -1517,6 +1539,7 @@
             pltpu.SemaphoreType.DMA((REAR_COPIES,)),
             pltpu.SemaphoreType.DMA((7,)),
         ]
+        + [pltpu.VMEM((2, 4) + up, low), pltpu.VMEM((2, 4) + up, low)]
         + [pltpu.VMEM(shape, low) for shape in buffers],
         compiler_params=pltpu.CompilerParams(
             collective_id=2, has_side_effects=True, vmem_limit_bytes=121 * 2**19
@@ -1588,10 +1611,10 @@
     )
     attended, heads_qkv, logsum, rows_all, gains, qkv, class_masks, mask_sums = outs[:8]
     normal_one, inverse_one, normed_two, active, d_branch, d_hidden = outs[8:14]
-    d_mix, d_second, d_attended, g_patch, g_class = outs[14:]
-    factors = (normed_two, active, d_branch, d_hidden, attended, d_mix)
+    d_mix, d_second, d_attended, *handed = outs[14:]
+    factors = (normed_two, active, d_branch, d_hidden, attended, d_mix, *handed)
     ending = (normal_one, inverse_one, d_second, gains)
-    grad_inputs, g_qkv, g_up, g_down, g_out, sums = rear(
+    grad_inputs, g_qkv, g_up, g_down, g_out, sums, g_patch, g_class = rear(
         live, d_attended, heads_qkv, logsum, rows_all, qkv, mask_sums, ending, factors, scaling
     )
     results = ending_copies(

time: 292 us -> 281 us (0.962)
  Pallas kernels: 287 us -> 276 us
    pallas_call x1, Pallas kernels: 180 us -> 171 us  [front(): pl.pallas_call(partial(front_kernel, scaling), out_shape=[jax.ShapeDtypeS...]
where the time goes in v1:
time: 281 us; the launch traced here: 280 us
  Pallas kernels  276 us (98%)
  local copies, waits for them, and re-layouts  3.48 us (1%)
    pallas_call x1, Pallas kernels, front(): pl.pallas_call(partial(front_kernel, scaling), out_shape=[jax.ShapeDtypeS...  171 us
    pallas_call x1, Pallas kernels, rear(): pl.pallas_call(partial(rear_kernel, scaling), out_shape=[jax.ShapeDtypeSt...  100 us

profile of v1, /device:TPU:0, one launch (start us, length us, event | category | flops | bytes accessed | tf_op | source)
XLA Modules:
  0.0 280.3 jit_solution(17866337765593618493)
XLA Ops:
  1.3 1.8 copy.21
  3.0 171.3 %front.1 = (bf16[256,1024]{1,0:T(8,128)(2,1)}, bf16[12,1024,64]{2,1,0:T(8,128)(2,1)}, f32[4,1,1024]{2,1,0:T(1,128)}, bf16[4,256,1024]{2,1,0:T(8,128)(2,1)}, f32[...) custom-call(s32[1]{0:T(128)S(6)} %add.3.refs_0_, ...), custom_call_target="tpu_custom_call" | custom-call | tf_op jit(solution)/shard_map/front/pallas_call | solution.py:1256
  174.4 100.5 %rear.1 = (f32[256,1024]{1,0:T(8,128)}, f32[32,3072]{1,0:T(8,128)}, f32[32,4096]{1,0:T(8,128)}, f32[128,1024]{1,0:T(8,128)}, f32[32,1024]{1,0:T(8,128)}, /*index...) custom-call(s32[1]{0:T(128)S(6)} %add.3.refs_0_, bf16[256,1024]{1,0:T(8,128)(2,1)} %get-tuple-element.48.refs_1_, ...), custom_call_target="tpu_custom_call" | custom-call | tf_op jit(solution)/shard_map/rear/pallas_call | solution.py:1511
  274.9 3.7 %ending.1 = (f32[256,150]{1,0:T(8,128)}, f32[256,1024]{1,0:T(8,128)}, f32[32,3072]{1,0:T(8,128)}, f32[32,1024]{1,0:T(8,128)}, f32[32,4096]{1,0:T(8,128)}, /*inde...) custom-call(f32[256,150]{1,0:T(8,128)} %get-tuple-element.47.refs_0_, ...), custom_call_target="tpu_custom_call" | custom-call | tf_op jit(solution)/shard_map/ending/pallas_call | solution.py:1573
  278.6 1.7 copy.22
